TPU v7x, 128 devices: a whole 4x4x4 slice. The times are simulated.
128 devices in a mesh: gx: 16 (over x, y), gy: 8 (over z, core).
Axes of the slice: x: 4, y: 4, z: 4, core: 2. Of those that a mesh axis runs over, the one named last changes fastest.
Arguments:
- field: float32 [256, 256, 1536], P('gx', 'gy'), may hold values from -24 to 24
- kappa: float32 [256, 256, 1536], P('gx', 'gy'), may hold values from 0.02 to 0.16
- history: float32 [126, 128, 64, 128], P(None, 'gx', 'gy'), may hold values from -2400 to 2400
Outputs:
- field_next: float32 [256, 256, 1536], P('gx', 'gy')
- basis: float32 [128, 128, 64, 128], P(None, 'gx', 'gy')
- factor: float32 [128, 128], replicated
All inputs are finite; a program needn't handle non-finite values.
Results may differ from a plain program's by a relative error of at most 0.00018.
Values sent between devices are 32-bit elements; how exact they have to be, the bound alone decides.
No kernel may reach another device: no remote copies, remote signals or barrier semaphores. Data moves between devices by JAX's collectives and lax.ppermute only.
A program may use at most 192 MiB of HBM per device.

v0:
```python
import jax
import jax.numpy as jnp
from jax import lax
from jax.sharding import PartitionSpec as P


def extended(block, sides, width):
    for axis, dim in sides:
        count = lax.axis_size(axis)
        forward = [(i, i + 1) for i in range(count - 1)]
        backward = [(target, source) for source, target in forward]
        low = lax.ppermute(
            lax.slice_in_dim(block, block.shape[dim] - width, None, axis=dim), axis, forward
        )
        high = lax.ppermute(lax.slice_in_dim(block, 0, width, axis=dim), axis, backward)
        block = jnp.concatenate([low, block, high], axis=dim)
    return block


def advance(field_pad, kappa_pad):
    field_z = jnp.pad(field_pad, ((0, 0), (0, 0), (1, 1)))
    kappa_z = jnp.pad(kappa_pad, ((0, 0), (0, 0), (1, 1)))
    centre = field_z[1:-1, 1:-1, 1:-1]
    kcentre = kappa_z[1:-1, 1:-1, 1:-1]
    places = [
        (slice(2, None), slice(1, -1), slice(1, -1)),
        (slice(None, -2), slice(1, -1), slice(1, -1)),
        (slice(1, -1), slice(2, None), slice(1, -1)),
        (slice(1, -1), slice(None, -2), slice(1, -1)),
        (slice(1, -1), slice(1, -1), slice(2, None)),
        (slice(1, -1), slice(1, -1), slice(None, -2)),
    ]
    change = jnp.zeros_like(centre)
    for place in places:
        change = change + 0.5 * (kcentre + kappa_z[place]) * (field_z[place] - centre)
    return centre + change


def sample(field):
    a, b, c = field.shape
    return field.reshape(a // 2, 2, b // 4, 4, c // 12, 12)[:, 0, :, 0, :, 0]


def body(field, kappa, history):
    both = jnp.stack([field, kappa])
    padded = extended(both, (("gx", 1), ("gy", 2)), 1)
    kappa_pad = padded[1]
    first = advance(padded[0], kappa_pad)
    first_pad = extended(first, (("gx", 0), ("gy", 1)), 1)
    second = advance(first_pad, kappa_pad)
    block = jnp.concatenate([history, sample(first)[None], sample(second)[None]], 0)
    shape = block.shape
    block = block.reshape(shape[0], -1)
    rows_all = block.shape[1] * lax.axis_size("gx") * lax.axis_size("gy")
    gram = jnp.einsum("ar,br->ab", block, block, precision=lax.Precision.HIGHEST) / rows_all
    total = lax.psum(gram, ("gx", "gy"))
    factor = jnp.linalg.cholesky(total).T
    basis = lax.linalg.triangular_solve(factor.T, block, left_side=True, lower=True)
    return (second, basis.reshape(shape), factor)


def solution(mesh):
    placed = (P("gx", "gy", None), P("gx", "gy", None), P(None, "gx", "gy", None))
    return jax.shard_map(
        body,
        mesh=mesh,
        in_specs=placed,
        out_specs=(P("gx", "gy", None), P(None, "gx", "gy", None), P()),
        check_vma=False,
    )
```

profile of v0, /device:TPU:1, one launch (start us, length us, event | category | flops | bytes accessed | tf_op | source)
XLA Modules:
  0.0 410.7 jit_solution(8603581438563554559)
XLA Ops:
  7.2 0.0 all-reduce.5.cloned.1.call-start
  7.2 0.0 copy-start
  7.2 0.0 copy-start.1
  7.2 1.4 pad_maximum_fusion.11
  8.7 4.2 %collective-permute-start = (f32[2,1,32,1536]{3,2,1,0:T(8,128)S(1)}, f32[2,1,32,1536]{3,2,1,0:T(8,128)S(1)}, u32[]{:S(2)}, u32[]{:S(2)}) collective-permute-start(f32[2,1,32,1536]{3,2,1,0:T(8,128)S(1)} %get-tuple-element.19), channel_id=1, source_target_pairs={{0,8},{8,16},{16,24},{24,32},{32,40},{40,48},{48,56},{56,64},{64,7... | collective-permute-start | bytes 1179656 | tf_op jit(solution)/shard_map/ppermute | solution.py:12
  12.8 1.3 collective-permute-start.1
  14.1 6.5 %collective-permute-done = f32[2,1,32,1536]{3,2,1,0:T(8,128)S(1)} collective-permute-done((f32[2,1,32,1536]{3,2,1,0:T(8,128)S(1)}, f32[2,1,32,1536]{3,2,1,0:T(8,128)S(1)}, u32[]{:S(2)}, u32[]{:S(2)}) %collective-permute-start) | collective-permute-done | bytes 393248 | tf_op jit(solution)/shard_map/ppermute | solution.py:12
  20.6 3.9 collective-permute-done.1
  24.4 0.0 copy-done
  24.4 0.0 copy-done.1
  24.5 0.3 pad_maximum_fusion.15
  24.8 5.2 %collective-permute-start.2 = (f32[2,18,1,1536]{3,2,1,0:T(1,128)S(1)}, f32[2,18,1,1536]{3,2,1,0:T(1,128)S(1)}, u32[]{:S(2)}, u32[]{:S(2)}) collective-permute-start(f32[2,18,1,1536]{3,2,1,0:T(1,128)S(1)} %get-tuple-element.17), channel_id=1, source_target_pairs={{0,1},{1,2},{2,3},{3,4},{4,5},{5,6},{6,7},{8,9},{9,10},{10,11},{11... | collective-permute-start | bytes 663560 | tf_op jit(solution)/shard_map/ppermute | solution.py:12
  30.1 1.9 collective-permute-start.3
  32.0 0.9 collective-permute-done.2
  32.9 4.4 %collective-permute-done.3 = f32[2,18,1,1536]{3,2,1,0:T(1,128)S(1)} collective-permute-done((f32[2,18,1,1536]{3,2,1,0:T(1,128)S(1)}, f32[2,18,1,1536]{3,2,1,0:T(1,128)S(1)}, u32[]{:S(2)}, u32[]{:S(2)}) %collective-permute-start.3) | collective-permute-done | bytes 221216 | tf_op jit(solution)/shard_map/ppermute | solution.py:15
  37.3 1.7 pad_maximum_fusion
  39.0 4.2 %slice_bitcast_fusion = (f32[18,34,1536]{2,1,0:T(8,128)}, f32[18,34,1536]{2,1,0:T(8,128)}) fusion(f32[2,18,34,1536]{3,2,1,0:T(8,128)S(1)} %pad_maximum_fusion), kind=kLoop, calls=%fused_computation.12 | loop fusion | bytes 15040512 | tf_op jit(solution)/shard_map/squeeze | solution.py:47
  43.2 28.3 %fusion.15 = f32[16,32,1536]{2,1,0:T(8,128)S(1)} fusion(f32[18,34,1536]{2,1,0:T(8,128)} %get-tuple-element.16, f32[18,34,1536]{2,1,0:T(8,128)} %get-tuple-element.15), kind=kLoop, calls=%fused_computation.29 | loop fusion | flops 23592960 | bytes 43450368 | tf_op jit(solution)/shard_map/add | solution.py:36
  71.5 0.0 copy-start.2
  71.6 1.6 collective-permute-start.4
  73.1 4.0 collective-permute-start.5
  77.1 1.1 collective-permute-done.4
  78.2 1.5 collective-permute-done.5
  79.7 0.2 pad_maximum_fusion.16
  79.9 0.7 copy.42
  80.6 1.9 collective-permute-start.6
  82.5 0.7 copy.44
  83.1 4.0 collective-permute-start.7
  87.2 0.0 copy-done.2
  87.2 4.3 %copy.50 = f32[126,8,8,128]{3,0,2,1:T(8,128)} copy(f32[126,8,8,128]{3,2,1,0:T(8,128)S(1)} %copy-done.2) | data formatting | bytes 8257536 | tf_op args[2]
  91.5 5.9 %copy.63 = f32[126,8,8,128]{0,3,2,1:T(8,128)} copy(f32[126,8,8,128]{3,2,1,0:T(8,128)} %param.5) | data formatting | bytes 8257536 | tf_op jit(solution)/shard_map/concatenate | solution.py:51
  97.5 38.1 %reshape.29 = f32[8,2,8,4,128,12]{5,4,3,2,1,0:T(8,128)} reshape(f32[16,32,1536]{2,1,0:T(8,128)S(1)} %fusion.15) | data formatting | bytes 6291456 | tf_op jit(solution)/shard_map/reshape | solution.py:41
  135.6 4.7 %slice.184 = f32[8,1,8,1,128,1]{5,4,3,2,1,0:T(8,128)} slice(f32[8,2,8,4,128,12]{5,4,3,2,1,0:T(8,128)} %reshape.29), slice={[0:8], [0:1], [0:8], [0:1], [0:128], [0:1]} | slice | bytes 65536 | tf_op jit(solution)/shard_map/slice | solution.py:41
  140.3 3.4 copy.64
  143.8 3.3 copy.54
  147.1 0.0 collective-permute-done.6
  147.1 1.0 copy.43
  148.1 0.0 collective-permute-done.7
  148.1 0.0 slice-start
  148.1 1.2 copy.45
  149.3 0.0 slice-start.1
  149.3 4.7 %select_maximum_fusion = f32[18,34,1538]{2,1,0:T(8,128)S(1)} fusion(f32[18,1,1536]{2,1,0:T(1,128)S(1)} %copy.43, f32[18,1,1536]{2,1,0:T(1,128)S(1)} %copy.45, f32[1,32,1536]{2,1,0:T(8,128)S(1)} %collective-permute-done.4, f32[16,32,1536]{2,1,0:T(8,128)S(1)} %fusion.15, f32[1,32,1536]{2,1,0:T(8,128)S(1)} %collective-permute-done.5), kind=kLoop, calls=%fused_computation.3 | loop fusion | flops 11295072 | bytes 7525152 | tf_op jit(solution)/shard_map/concatenate | solution.py:16
  154.0 0.0 slice-done
  154.0 0.0 slice-done.1
  154.0 12.9 %fusion.20 = f32[16,32,1536]{2,1,0:T(8,128)} fusion(f32[16,32,1536]{2,1,0:T(8,128)S(1)} %fusion.15, f32[18,34,1538]{2,1,0:T(8,128)S(1)} %select_maximum_fusion, f32[18,1,1536]{2,1,0:T(1,128)S(1)} %copy.45, f32[1,32,1536]{2,1,0:T(8,128)S(1)} %collective-permute-done.4, f32[1,32,1536]{2,1,0:T(8,128)S(1)} %collective-permute-done.5, ...), kind=kLoop, calls=%fused_computation.35 | loop fusion | flops 29884416 | bytes 33349632 | tf_op jit(solution)/shard_map/add | solution.py:36
  167.0 39.1 %reshape.30 = f32[8,2,8,4,128,12]{5,4,3,2,1,0:T(8,128)} reshape(f32[16,32,1536]{2,1,0:T(8,128)} %fusion.20) | data formatting | bytes 6291456 | tf_op jit(solution)/shard_map/reshape | solution.py:41
  206.1 4.7 %slice.185 = f32[8,1,8,1,128,1]{5,4,3,2,1,0:T(8,128)} slice(f32[8,2,8,4,128,12]{5,4,3,2,1,0:T(8,128)} %reshape.30), slice={[0:8], [0:1], [0:8], [0:1], [0:128], [0:1]} | slice | bytes 65536 | tf_op jit(solution)/shard_map/slice | solution.py:41
  210.8 0.0 copy-start.3
  210.8 2.8 copy.65
  213.7 0.0 copy-done.3
  213.7 7.7 %fusion.48 = f32[128,128]{0,1:T(8,128)} fusion(f32[1,8,8,128]{3,0,2,1:T(1,128)S(1)} %bitcast.44, f32[1,8,8,128]{3,0,2,1:T(1,128)S(1)} %bitcast.43, f32[126,8,8,128]{3,0,2,1:T(8,128)} %copy.50), kind=kOutput, calls=%fused_computation.78 | convolution fusion | flops 1612726272 | bytes 4259840 | tf_op jit(solution)/shard_map/ar,br->ab/dot_general | solution.py:55
  221.4 0.0 all-reduce.5.cloned.1.call-update
  221.4 2.8 copy.55
  224.2 8.9 %pad_maximum_fusion.1 = f32[128,8192]{0,1:T(8,128)} fusion(f32[1,8192]{0,1:T(8,128)} %copy.55, f32[1,8192]{0,1:T(8,128)} %copy.54, f32[126,8192]{0,1:T(8,128)} %bitcast.40), kind=kLoop, calls=%fused_computation.20 | loop fusion | flops 2097152 | bytes 8388608 | tf_op jit(solution)/shard_map/concatenate | solution.py:51
  233.1 135.0 %all-reduce.5.cloned.1.call-done = f32[128,128]{0,1:T(8,128)} async-done(((f32[128,128]{0,1:T(8,128)}), f32[128,128]{0,1:T(8,128)}) %all-reduce.5.cloned.1.call-update) | async-done | bytes 65552 | tf_op jit(solution)/shard_map/psum | solution.py:56
  368.1 0.9 copy.52
  369.0 0.9 fusion.53
  369.9 11.7 %cholesky.16 = f32[128,128]{1,0:T(8,128)S(1)} custom-call(f32[128,128]{1,0:T(8,128)S(1)} %fusion.53), custom_call_target="Cholesky" | custom-call | tf_op jit(solution)/shard_map/jit(cholesky)/cholesky | solution.py:57
  381.6 0.6 compare_reduce_fusion
  382.3 0.7 fusion.54
  382.9 9.8 %custom-call.6 = f32[1,128,128]{1,2,0:T(8,128)S(1)} custom-call(f32[1,128,128]{2,1,0:T(8,128)S(1)} %get-tuple-element.26), custom_call_target="InvertDiagBlocksLowerTriangular" | custom-call | tf_op jit(solution)/shard_map/triangular_solve | solution.py:58
  392.7 5.7 %fusion.51 = f32[128,8,8,128]{3,0,2,1:T(8,128)S(1)} fusion(f32[8,8,128,128]{3,2,1,0:T(8,128)} %bitcast.41, f32[1,128,128]{1,2,0:T(8,128)S(1)} %custom-call.6), kind=kOutput, calls=%fused_computation.88 | convolution fusion | flops 1610612736 | bytes 8454144 | tf_op jit(solution)/shard_map/triangular_solve | solution.py:58
  398.4 4.4 %copy.57 = f32[128,8,8,128]{3,2,1,0:T(8,128)} copy(f32[128,8,8,128]{3,0,2,1:T(8,128)S(1)} %fusion.51) | data formatting | bytes 8388608
  402.9 0.7 copy.58
  (3 shorter events, 0.1 us)
Async XLA Ops:
  7.2 360.9 %all-reduce.5.cloned.1.call-start = ((), (), s32[]{:S(2)}) async-start(), calls=%async_computation | async-start | bytes 131072 | tf_op jit(solution)/shard_map/psum | solution.py:56
  7.2 17.2 %copy-start = (f32[16,32,1536]{2,1,0:T(8,128)S(1)}, f32[16,32,1536]{2,1,0:T(8,128)}, u32[]{:S(2)}) copy-start(f32[16,32,1536]{2,1,0:T(8,128)} %param.4) | copy-start | bytes 9437188
  7.2 17.2 %copy-start.1 = (f32[16,32,1536]{2,1,0:T(8,128)S(1)}, f32[16,32,1536]{2,1,0:T(8,128)}, u32[]{:S(2)}) copy-start(f32[16,32,1536]{2,1,0:T(8,128)} %param.3) | copy-start | bytes 9437188
  8.7 11.9 %collective-permute-start = (f32[2,1,32,1536]{3,2,1,0:T(8,128)S(1)}, f32[2,1,32,1536]{3,2,1,0:T(8,128)S(1)}, u32[]{:S(2)}, u32[]{:S(2)}) collective-permute-start(f32[2,1,32,1536]{3,2,1,0:T(8,128)S(1)} %get-tuple-element.19), channel_id=1, source_target_pairs={{0,8},{8,16},{16,24},{24,32},{32,40},{40,48},{48,56},{56,64},{64,7... | collective-permute-start | bytes 1179656 | tf_op jit(solution)/shard_map/ppermute | solution.py:12
  12.8 11.6 %collective-permute-start.1 = (f32[2,1,32,1536]{3,2,1,0:T(8,128)S(1)}, f32[2,1,32,1536]{3,2,1,0:T(8,128)S(1)}, u32[]{:S(2)}, u32[]{:S(2)}) collective-permute-start(f32[2,1,32,1536]{3,2,1,0:T(8,128)S(1)} %get-tuple-element.20), channel_id=1, source_target_pairs={{8,0},{16,8},{24,16},{32,24},{40,32},{48,40},{56,48},{64,56},{72,6... | collective-permute-start | bytes 1179656 | tf_op jit(solution)/shard_map/ppermute | solution.py:15
  24.8 8.1 %collective-permute-start.2 = (f32[2,18,1,1536]{3,2,1,0:T(1,128)S(1)}, f32[2,18,1,1536]{3,2,1,0:T(1,128)S(1)}, u32[]{:S(2)}, u32[]{:S(2)}) collective-permute-start(f32[2,18,1,1536]{3,2,1,0:T(1,128)S(1)} %get-tuple-element.17), channel_id=1, source_target_pairs={{0,1},{1,2},{2,3},{3,4},{4,5},{5,6},{6,7},{8,9},{9,10},{10,11},{11... | collective-permute-start | bytes 663560 | tf_op jit(solution)/shard_map/ppermute | solution.py:12
  30.1 7.3 %collective-permute-start.3 = (f32[2,18,1,1536]{3,2,1,0:T(1,128)S(1)}, f32[2,18,1,1536]{3,2,1,0:T(1,128)S(1)}, u32[]{:S(2)}, u32[]{:S(2)}) collective-permute-start(f32[2,18,1,1536]{3,2,1,0:T(1,128)S(1)} %get-tuple-element.18), channel_id=1, source_target_pairs={{1,0},{2,1},{3,2},{4,3},{5,4},{6,5},{7,6},{9,8},{10,9},{11,10},{12... | collective-permute-start | bytes 663560 | tf_op jit(solution)/shard_map/ppermute | solution.py:15
  71.5 15.7 %copy-start.2 = (f32[126,8,8,128]{3,2,1,0:T(8,128)S(1)}, f32[126,8,8,128]{3,2,1,0:T(8,128)}, u32[]{:S(2)}) copy-start(f32[126,8,8,128]{3,2,1,0:T(8,128)} %param.5) | copy-start | bytes 12386308
  71.6 6.7 %collective-permute-start.4 = (f32[1,32,1536]{2,1,0:T(8,128)S(1)}, f32[1,32,1536]{2,1,0:T(8,128)S(1)}, u32[]{:S(2)}, u32[]{:S(2)}) collective-permute-start(f32[1,32,1536]{2,1,0:T(8,128)S(1)} %get-tuple-element.24), channel_id=1, source_target_pairs={{8,0},{16,8},{24,16},{32,24},{40,32},{48,40},{56,48},{64,56},{72,6... | collective-permute-start | bytes 589832 | tf_op jit(solution)/shard_map/ppermute | solution.py:15
  73.1 6.6 %collective-permute-start.5 = (f32[1,32,1536]{2,1,0:T(8,128)S(1)}, f32[1,32,1536]{2,1,0:T(8,128)S(1)}, u32[]{:S(2)}, u32[]{:S(2)}) collective-permute-start(f32[1,32,1536]{2,1,0:T(8,128)S(1)} %get-tuple-element.23), channel_id=1, source_target_pairs={{0,8},{8,16},{16,24},{24,32},{32,40},{40,48},{48,56},{56,64},{64,7... | collective-permute-start | bytes 589832 | tf_op jit(solution)/shard_map/ppermute | solution.py:12
  80.6 66.5 %collective-permute-start.6 = (f32[18,1,1536]{2,0,1:T(8,128)}, f32[18,1,1536]{2,0,1:T(8,128)}, u32[]{:S(2)}, u32[]{:S(2)}) collective-permute-start(f32[18,1,1536]{2,0,1:T(8,128)} %copy.42), channel_id=1, source_target_pairs={{1,0},{2,1},{3,2},{4,3},{5,4},{6,5},{7,6},{9,8},{10,9},{11,10},{12... | collective-permute-start | bytes 331784 | tf_op jit(solution)/shard_map/ppermute | solution.py:15
  83.1 65.0 %collective-permute-start.7 = (f32[18,1,1536]{2,0,1:T(8,128)}, f32[18,1,1536]{2,0,1:T(8,128)}, u32[]{:S(2)}, u32[]{:S(2)}) collective-permute-start(f32[18,1,1536]{2,0,1:T(8,128)} %copy.44), channel_id=1, source_target_pairs={{0,1},{1,2},{2,3},{3,4},{4,5},{5,6},{6,7},{8,9},{9,10},{10,11},{11... | collective-permute-start | bytes 331784 | tf_op jit(solution)/shard_map/ppermute | solution.py:12
  148.1 5.9 %slice-start = ((s8[4423680]{0:T(1024)(128)(4,1)}), s8[4194304]{0:T(1024)(128)(4,1)S(1)}, s32[]{:S(2)}) async-start(s8[4423680]{0:T(1024)(128)(4,1)} %bitcast.32), calls=%async_computation.1 | async-start | bytes 8388608
  149.3 4.7 %slice-start.1 = ((s8[4423680]{0:T(1024)(128)(4,1)}), s8[229376]{0:T(1024)(128)(4,1)S(1)}, s32[]{:S(2)}) async-start(s8[4423680]{0:T(1024)(128)(4,1)} %bitcast.32), calls=%async_computation.2 | async-start | bytes 458752
  210.8 2.8 copy-start.3
Sparse Core Ops, SparseCore 0:
  221.5 146.5 all-reduce.4
where the time goes:
time: 419 us; the launch traced here: 411 us
  waiting for transfers between devices  153 us (37%)
  local copies, waits for them, and re-layouts  123 us (29%)
  other arithmetic  82.1 us (20%)
  starting transfers between devices  24.2 us (6%)
  between operations  14.5 us (3%)
  matrix products  13.4 us (3%)
    psum x1, waiting for transfers between devices, body(): total = lax.psum(gram, ('gx', 'gy'))  135 us
    reshape x2, local copies, waits for them, and re-layouts, sample(): return field.reshape(a // 2, 2, b // 4, 4, c // 12, 12)[:, 0, :, 0, :, 0]  77.3 us
    add x2, other arithmetic, advance(): return centre + change  41.3 us
    ppermute x4, starting transfers between devices, extended(): lax.ppermute(lax.slice_in_dim(block, block.shape[dim] - width, None, axis...  17.4 us
    unnamed x17, local copies, waits for them, and re-layouts  15.8 us
    another operation x3, other arithmetic, body(): factor = jnp.linalg.cholesky(total).T  12.4 us
    concatenate x3, local copies, waits for them, and re-layouts, body(): jnp.concatenate([history, sample(first)[None], sample(second)[None]], 0)  12.1 us
    another operation x1, other arithmetic, body(): lax.linalg.triangular_solve(factor.T, block, left_side=True, lower=True)  9.81 us
  transfers between devices with their start and end apart: 9, of which 7 were waited for; matrix products, arithmetic and copies ran while one was open for 18% of the time, Pallas kernels for 0%

commit v1 on v0

--- a/solution.py
+++ b/solution.py
@@ -53,7 +53,9 @@
     block = block.reshape(shape[0], -1)
     rows_all = block.shape[1] * lax.axis_size("gx") * lax.axis_size("gy")
     gram = jnp.einsum("ar,br->ab", block, block, precision=lax.Precision.HIGHEST) / rows_all
-    total = lax.psum(gram, ("gx", "gy"))
+    total = gram
+    for mesh_axis in ("gx", "gy"):
+        total = lax.psum(total, mesh_axis)
     factor = jnp.linalg.cholesky(total).T
     basis = lax.linalg.triangular_solve(factor.T, block, left_side=True, lower=True)
     return (second, basis.reshape(shape), factor)

time: 419 us -> 422 us (level)
  local copies, waits for them, and re-layouts: 123 us -> 133 us
  waiting for transfers between devices: 153 us -> 147 us
    unnamed x17, local copies, waits for them, and re-layouts: 15.8 us -> 26.7 us
    psum x1 -> x2, waiting for transfers between devices: 135 us -> 128 us  [body(): total = lax.psum(total, mesh_axis)]
  transfers between devices with their start and end apart: 9 -> 10, of which waited for: 7 -> 8; matrix products, arithmetic and copies ran while one was open for 18% -> 17% of each run, Pallas kernels for 0% -> 0%
where the time goes in v1:
time: 422 us; the launch traced here: 414 us
  waiting for transfers between devices  147 us (35%)
  local copies, waits for them, and re-layouts  133 us (32%)
  other arithmetic  82.1 us (19%)
  starting transfers between devices  24.6 us (6%)
  between operations  14.5 us (3%)
  matrix products  13.4 us (3%)
    psum x2, waiting for transfers between devices, body(): total = lax.psum(total, mesh_axis)  128 us
    reshape x2, local copies, waits for them, and re-layouts, sample(): return field.reshape(a // 2, 2, b // 4, 4, c // 12, 12)[:, 0, :, 0, :, 0]  77.3 us
    add x2, other arithmetic, advance(): return centre + change  41.3 us
    unnamed x17, local copies, waits for them, and re-layouts  26.7 us
    ppermute x4, starting transfers between devices, extended(): lax.ppermute(lax.slice_in_dim(block, block.shape[dim] - width, None, axis...  17.8 us
    another operation x3, other arithmetic, body(): factor = jnp.linalg.cholesky(total).T  12.4 us
    concatenate x3, local copies, waits for them, and re-layouts, body(): jnp.concatenate([history, sample(first)[None], sample(second)[None]], 0)  10.8 us
    another operation x1, other arithmetic, body(): lax.linalg.triangular_solve(factor.T, block, left_side=True, lower=True)  9.81 us
  transfers between devices with their start and end apart: 10, of which 8 were waited for; matrix products, arithmetic and copies ran while one was open for 17% of the time, Pallas kernels for 0%

profile of v1, /device:TPU:1, one launch (start us, length us, event | category | flops | bytes accessed | tf_op | source)
XLA Modules:
  0.0 414.0 jit_solution(14224669833766496601)
XLA Ops:
  7.2 0.0 all-reduce.6.cloned.1.call-start
  7.2 0.0 copy-start
  7.2 0.0 copy-start.1
  7.2 1.4 pad_maximum_fusion.11
  8.7 4.2 %collective-permute-start = (f32[2,1,32,1536]{3,2,1,0:T(8,128)S(1)}, f32[2,1,32,1536]{3,2,1,0:T(8,128)S(1)}, u32[]{:S(2)}, u32[]{:S(2)}) collective-permute-start(f32[2,1,32,1536]{3,2,1,0:T(8,128)S(1)} %get-tuple-element.19), channel_id=1, source_target_pairs={{0,8},{8,16},{16,24},{24,32},{32,40},{40,48},{48,56},{56,64},{64,7... | collective-permute-start | bytes 1179656 | tf_op jit(solution)/shard_map/ppermute | solution.py:12
  12.8 1.3 collective-permute-start.1
  14.1 6.5 %collective-permute-done = f32[2,1,32,1536]{3,2,1,0:T(8,128)S(1)} collective-permute-done((f32[2,1,32,1536]{3,2,1,0:T(8,128)S(1)}, f32[2,1,32,1536]{3,2,1,0:T(8,128)S(1)}, u32[]{:S(2)}, u32[]{:S(2)}) %collective-permute-start) | collective-permute-done | bytes 393248 | tf_op jit(solution)/shard_map/ppermute | solution.py:12
  20.6 3.9 collective-permute-done.1
  24.4 0.0 copy-done
  24.4 0.0 copy-done.1
  24.5 0.3 pad_maximum_fusion.15
  24.8 5.2 %collective-permute-start.2 = (f32[2,18,1,1536]{3,2,1,0:T(1,128)S(1)}, f32[2,18,1,1536]{3,2,1,0:T(1,128)S(1)}, u32[]{:S(2)}, u32[]{:S(2)}) collective-permute-start(f32[2,18,1,1536]{3,2,1,0:T(1,128)S(1)} %get-tuple-element.17), channel_id=1, source_target_pairs={{0,1},{1,2},{2,3},{3,4},{4,5},{5,6},{6,7},{8,9},{9,10},{10,11},{11... | collective-permute-start | bytes 663560 | tf_op jit(solution)/shard_map/ppermute | solution.py:12
  30.1 1.9 collective-permute-start.3
  32.0 0.9 collective-permute-done.2
  32.9 4.4 %collective-permute-done.3 = f32[2,18,1,1536]{3,2,1,0:T(1,128)S(1)} collective-permute-done((f32[2,18,1,1536]{3,2,1,0:T(1,128)S(1)}, f32[2,18,1,1536]{3,2,1,0:T(1,128)S(1)}, u32[]{:S(2)}, u32[]{:S(2)}) %collective-permute-start.3) | collective-permute-done | bytes 221216 | tf_op jit(solution)/shard_map/ppermute | solution.py:15
  37.3 1.7 pad_maximum_fusion
  39.0 4.2 %slice_bitcast_fusion = (f32[18,34,1536]{2,1,0:T(8,128)}, f32[18,34,1536]{2,1,0:T(8,128)}) fusion(f32[2,18,34,1536]{3,2,1,0:T(8,128)S(1)} %pad_maximum_fusion), kind=kLoop, calls=%fused_computation.12 | loop fusion | bytes 15040512 | tf_op jit(solution)/shard_map/squeeze | solution.py:47
  43.2 28.3 %fusion.15 = f32[16,32,1536]{2,1,0:T(8,128)S(1)} fusion(f32[18,34,1536]{2,1,0:T(8,128)} %get-tuple-element.16, f32[18,34,1536]{2,1,0:T(8,128)} %get-tuple-element.15), kind=kLoop, calls=%fused_computation.29 | loop fusion | flops 23592960 | bytes 43450368 | tf_op jit(solution)/shard_map/add | solution.py:36
  71.5 0.0 copy-start.2
  71.6 1.6 collective-permute-start.4
  73.1 4.0 collective-permute-start.5
  77.1 1.1 collective-permute-done.4
  78.2 1.5 collective-permute-done.5
  79.7 0.2 pad_maximum_fusion.16
  79.9 0.7 copy.42
  80.6 1.9 collective-permute-start.6
  82.5 0.7 copy.44
  83.1 4.4 %collective-permute-start.7 = (f32[18,1,1536]{2,0,1:T(8,128)}, f32[18,1,1536]{2,0,1:T(8,128)}, u32[]{:S(2)}, u32[]{:S(2)}) collective-permute-start(f32[18,1,1536]{2,0,1:T(8,128)} %copy.44), channel_id=1, source_target_pairs={{0,1},{1,2},{2,3},{3,4},{4,5},{5,6},{6,7},{8,9},{9,10},{10,11},{11... | collective-permute-start | bytes 331784 | tf_op jit(solution)/shard_map/ppermute | solution.py:12
  87.6 4.4 %copy.50 = f32[126,8,8,128]{3,0,2,1:T(8,128)} copy(f32[126,8,8,128]{3,2,1,0:T(8,128)S(1)} %copy-done.2) | data formatting | bytes 8257536 | tf_op args[2]
  92.0 38.1 %reshape.29 = f32[8,2,8,4,128,12]{5,4,3,2,1,0:T(8,128)} reshape(f32[16,32,1536]{2,1,0:T(8,128)S(1)} %fusion.15) | data formatting | bytes 6291456 | tf_op jit(solution)/shard_map/reshape | solution.py:41
  130.1 4.7 %slice.184 = f32[8,1,8,1,128,1]{5,4,3,2,1,0:T(8,128)} slice(f32[8,2,8,4,128,12]{5,4,3,2,1,0:T(8,128)} %reshape.29), slice={[0:8], [0:1], [0:8], [0:1], [0:128], [0:1]} | slice | bytes 65536 | tf_op jit(solution)/shard_map/slice | solution.py:41
  134.8 3.4 copy.64
  138.2 0.0 collective-permute-done.6
  138.3 1.0 copy.43
  139.3 0.0 collective-permute-done.7
  139.3 0.0 slice-start
  139.3 1.2 copy.45
  140.5 0.0 slice-start.1
  140.5 4.7 %select_maximum_fusion = f32[18,34,1538]{2,1,0:T(8,128)S(1)} fusion(f32[18,1,1536]{2,1,0:T(1,128)S(1)} %copy.43, f32[18,1,1536]{2,1,0:T(1,128)S(1)} %copy.45, f32[1,32,1536]{2,1,0:T(8,128)S(1)} %collective-permute-done.4, f32[16,32,1536]{2,1,0:T(8,128)S(1)} %fusion.15, f32[1,32,1536]{2,1,0:T(8,128)S(1)} %collective-permute-done.5), kind=kLoop, calls=%fused_computation.3 | loop fusion | flops 11295072 | bytes 7525152 | tf_op jit(solution)/shard_map/concatenate | solution.py:16
  145.2 0.0 slice-done
  145.2 0.0 slice-done.1
  145.2 12.9 %fusion.20 = f32[16,32,1536]{2,1,0:T(8,128)} fusion(f32[16,32,1536]{2,1,0:T(8,128)S(1)} %fusion.15, f32[18,34,1538]{2,1,0:T(8,128)S(1)} %select_maximum_fusion, f32[18,1,1536]{2,1,0:T(1,128)S(1)} %copy.45, f32[1,32,1536]{2,1,0:T(8,128)S(1)} %collective-permute-done.4, f32[1,32,1536]{2,1,0:T(8,128)S(1)} %collective-permute-done.5, ...), kind=kLoop, calls=%fused_computation.35 | loop fusion | flops 29884416 | bytes 33349632 | tf_op jit(solution)/shard_map/add | solution.py:36
  158.1 39.1 %reshape.30 = f32[8,2,8,4,128,12]{5,4,3,2,1,0:T(8,128)} reshape(f32[16,32,1536]{2,1,0:T(8,128)} %fusion.20) | data formatting | bytes 6291456 | tf_op jit(solution)/shard_map/reshape | solution.py:41
  197.3 4.7 %slice.185 = f32[8,1,8,1,128,1]{5,4,3,2,1,0:T(8,128)} slice(f32[8,2,8,4,128,12]{5,4,3,2,1,0:T(8,128)} %reshape.30), slice={[0:8], [0:1], [0:8], [0:1], [0:128], [0:1]} | slice | bytes 65536 | tf_op jit(solution)/shard_map/slice | solution.py:41
  202.0 13.7 %copy.65 = f32[8,1,8,1,128,1]{4,2,0,5,3,1:T(8,128)S(1)} copy(f32[8,1,8,1,128,1]{5,4,3,2,1,0:T(8,128)} %slice.185) | data formatting | bytes 65536
  215.6 7.7 %fusion.48 = f32[128,128]{0,1:T(8,128)} fusion(f32[1,8,8,128]{3,0,2,1:T(1,128)S(1)} %bitcast.44, f32[1,8,8,128]{3,0,2,1:T(1,128)S(1)} %bitcast.42, f32[126,8,8,128]{3,0,2,1:T(8,128)} %copy.50), kind=kOutput, calls=%fused_computation.78 | convolution fusion | flops 1612726272 | bytes 4259840 | tf_op jit(solution)/shard_map/ar,br->ab/dot_general | solution.py:55
  223.4 0.0 all-reduce.6.cloned.1.call-update
  223.4 0.0 all-reduce.8.cloned.1.call-start
  223.4 5.4 %copy.63 = f32[126,8,8,128]{0,3,2,1:T(8,128)} copy(f32[126,8,8,128]{3,2,1,0:T(8,128)} %param.5) | data formatting | bytes 8257536 | tf_op jit(solution)/shard_map/concatenate | solution.py:51
  228.9 2.7 copy.54
  231.5 2.7 copy.55
  234.2 76.0 %all-reduce.6.cloned.1.call-done = f32[128,128]{0,1:T(8,128)} async-done(((f32[128,128]{0,1:T(8,128)}), f32[128,128]{0,1:T(8,128)}) %all-reduce.6.cloned.1.call-update) | async-done | bytes 65552 | tf_op jit(solution)/shard_map/psum | solution.py:58
  310.2 0.0 all-reduce.8.cloned.1.call-update
  310.3 8.9 %pad_maximum_fusion.1 = f32[128,8192]{0,1:T(8,128)} fusion(f32[1,8192]{0,1:T(8,128)} %copy.55, f32[1,8192]{0,1:T(8,128)} %copy.54, f32[126,8192]{0,1:T(8,128)} %bitcast.41), kind=kLoop, calls=%fused_computation.20 | loop fusion | flops 2097152 | bytes 8388608 | tf_op jit(solution)/shard_map/concatenate | solution.py:51
  319.1 52.3 %all-reduce.8.cloned.1.call-done = f32[128,128]{0,1:T(8,128)} async-done(((f32[128,128]{0,1:T(8,128)}), f32[128,128]{0,1:T(8,128)}) %all-reduce.8.cloned.1.call-update) | async-done | bytes 65552 | tf_op jit(solution)/shard_map/psum | solution.py:58
  371.5 0.9 copy.52
  372.4 0.9 fusion.53
  373.3 11.7 %cholesky.16 = f32[128,128]{1,0:T(8,128)S(1)} custom-call(f32[128,128]{1,0:T(8,128)S(1)} %fusion.53), custom_call_target="Cholesky" | custom-call | tf_op jit(solution)/shard_map/jit(cholesky)/cholesky | solution.py:59
  385.0 0.6 compare_reduce_fusion
  385.6 0.7 fusion.54
  386.3 9.8 %custom-call.6 = f32[1,128,128]{1,2,0:T(8,128)S(1)} custom-call(f32[1,128,128]{2,1,0:T(8,128)S(1)} %get-tuple-element.26), custom_call_target="InvertDiagBlocksLowerTriangular" | custom-call | tf_op jit(solution)/shard_map/triangular_solve | solution.py:60
  396.1 5.7 %fusion.51 = f32[128,8,8,128]{3,0,2,1:T(8,128)S(1)} fusion(f32[8,8,128,128]{3,2,1,0:T(8,128)} %bitcast.40, f32[1,128,128]{1,2,0:T(8,128)S(1)} %custom-call.6), kind=kOutput, calls=%fused_computation.88 | convolution fusion | flops 1610612736 | bytes 8454144 | tf_op jit(solution)/shard_map/triangular_solve | solution.py:60
  401.8 4.4 %copy.57 = f32[128,8,8,128]{3,2,1,0:T(8,128)} copy(f32[128,8,8,128]{3,0,2,1:T(8,128)S(1)} %fusion.51) | data formatting | bytes 8388608
  406.2 0.7 copy.58
  (6 shorter events, 0.1 us)
Async XLA Ops:
  7.2 303.1 %all-reduce.6.cloned.1.call-start = ((), (), s32[]{:S(2)}) async-start(), calls=%async_computation | async-start | bytes 131072 | tf_op jit(solution)/shard_map/psum | solution.py:58
  7.2 17.2 %copy-start = (f32[16,32,1536]{2,1,0:T(8,128)S(1)}, f32[16,32,1536]{2,1,0:T(8,128)}, u32[]{:S(2)}) copy-start(f32[16,32,1536]{2,1,0:T(8,128)} %param.4) | copy-start | bytes 9437188
  7.2 17.2 %copy-start.1 = (f32[16,32,1536]{2,1,0:T(8,128)S(1)}, f32[16,32,1536]{2,1,0:T(8,128)}, u32[]{:S(2)}) copy-start(f32[16,32,1536]{2,1,0:T(8,128)} %param.3) | copy-start | bytes 9437188
  8.7 11.9 %collective-permute-start = (f32[2,1,32,1536]{3,2,1,0:T(8,128)S(1)}, f32[2,1,32,1536]{3,2,1,0:T(8,128)S(1)}, u32[]{:S(2)}, u32[]{:S(2)}) collective-permute-start(f32[2,1,32,1536]{3,2,1,0:T(8,128)S(1)} %get-tuple-element.19), channel_id=1, source_target_pairs={{0,8},{8,16},{16,24},{24,32},{32,40},{40,48},{48,56},{56,64},{64,7... | collective-permute-start | bytes 1179656 | tf_op jit(solution)/shard_map/ppermute | solution.py:12
  12.8 11.6 %collective-permute-start.1 = (f32[2,1,32,1536]{3,2,1,0:T(8,128)S(1)}, f32[2,1,32,1536]{3,2,1,0:T(8,128)S(1)}, u32[]{:S(2)}, u32[]{:S(2)}) collective-permute-start(f32[2,1,32,1536]{3,2,1,0:T(8,128)S(1)} %get-tuple-element.20), channel_id=1, source_target_pairs={{8,0},{16,8},{24,16},{32,24},{40,32},{48,40},{56,48},{64,56},{72,6... | collective-permute-start | bytes 1179656 | tf_op jit(solution)/shard_map/ppermute | solution.py:15
  24.8 8.1 %collective-permute-start.2 = (f32[2,18,1,1536]{3,2,1,0:T(1,128)S(1)}, f32[2,18,1,1536]{3,2,1,0:T(1,128)S(1)}, u32[]{:S(2)}, u32[]{:S(2)}) collective-permute-start(f32[2,18,1,1536]{3,2,1,0:T(1,128)S(1)} %get-tuple-element.17), channel_id=1, source_target_pairs={{0,1},{1,2},{2,3},{3,4},{4,5},{5,6},{6,7},{8,9},{9,10},{10,11},{11... | collective-permute-start | bytes 663560 | tf_op jit(solution)/shard_map/ppermute | solution.py:12
  30.1 7.3 %collective-permute-start.3 = (f32[2,18,1,1536]{3,2,1,0:T(1,128)S(1)}, f32[2,18,1,1536]{3,2,1,0:T(1,128)S(1)}, u32[]{:S(2)}, u32[]{:S(2)}) collective-permute-start(f32[2,18,1,1536]{3,2,1,0:T(1,128)S(1)} %get-tuple-element.18), channel_id=1, source_target_pairs={{1,0},{2,1},{3,2},{4,3},{5,4},{6,5},{7,6},{9,8},{10,9},{11,10},{12... | collective-permute-start | bytes 663560 | tf_op jit(solution)/shard_map/ppermute | solution.py:15
  71.5 16.0 %copy-start.2 = (f32[126,8,8,128]{3,2,1,0:T(8,128)S(1)}, f32[126,8,8,128]{3,2,1,0:T(8,128)}, u32[]{:S(2)}) copy-start(f32[126,8,8,128]{3,2,1,0:T(8,128)} %param.5) | copy-start | bytes 12386308
  71.6 6.7 %collective-permute-start.4 = (f32[1,32,1536]{2,1,0:T(8,128)S(1)}, f32[1,32,1536]{2,1,0:T(8,128)S(1)}, u32[]{:S(2)}, u32[]{:S(2)}) collective-permute-start(f32[1,32,1536]{2,1,0:T(8,128)S(1)} %get-tuple-element.24), channel_id=1, source_target_pairs={{8,0},{16,8},{24,16},{32,24},{40,32},{48,40},{56,48},{64,56},{72,6... | collective-permute-start | bytes 589832 | tf_op jit(solution)/shard_map/ppermute | solution.py:15
  73.1 6.6 %collective-permute-start.5 = (f32[1,32,1536]{2,1,0:T(8,128)S(1)}, f32[1,32,1536]{2,1,0:T(8,128)S(1)}, u32[]{:S(2)}, u32[]{:S(2)}) collective-permute-start(f32[1,32,1536]{2,1,0:T(8,128)S(1)} %get-tuple-element.23), channel_id=1, source_target_pairs={{0,8},{8,16},{16,24},{24,32},{32,40},{40,48},{48,56},{56,64},{64,7... | collective-permute-start | bytes 589832 | tf_op jit(solution)/shard_map/ppermute | solution.py:12
  80.6 57.7 %collective-permute-start.6 = (f32[18,1,1536]{2,0,1:T(8,128)}, f32[18,1,1536]{2,0,1:T(8,128)}, u32[]{:S(2)}, u32[]{:S(2)}) collective-permute-start(f32[18,1,1536]{2,0,1:T(8,128)} %copy.42), channel_id=1, source_target_pairs={{1,0},{2,1},{3,2},{4,3},{5,4},{6,5},{7,6},{9,8},{10,9},{11,10},{12... | collective-permute-start | bytes 331784 | tf_op jit(solution)/shard_map/ppermute | solution.py:15
  83.1 56.1 %collective-permute-start.7 = (f32[18,1,1536]{2,0,1:T(8,128)}, f32[18,1,1536]{2,0,1:T(8,128)}, u32[]{:S(2)}, u32[]{:S(2)}) collective-permute-start(f32[18,1,1536]{2,0,1:T(8,128)} %copy.44), channel_id=1, source_target_pairs={{0,1},{1,2},{2,3},{3,4},{4,5},{5,6},{6,7},{8,9},{9,10},{10,11},{11... | collective-permute-start | bytes 331784 | tf_op jit(solution)/shard_map/ppermute | solution.py:12
  139.3 5.9 %slice-start = ((s8[4423680]{0:T(1024)(128)(4,1)}), s8[4194304]{0:T(1024)(128)(4,1)S(1)}, s32[]{:S(2)}) async-start(s8[4423680]{0:T(1024)(128)(4,1)} %bitcast.32), calls=%async_computation.2 | async-start | bytes 8388608
  140.5 4.7 %slice-start.1 = ((s8[4423680]{0:T(1024)(128)(4,1)}), s8[229376]{0:T(1024)(128)(4,1)S(1)}, s32[]{:S(2)}) async-start(s8[4423680]{0:T(1024)(128)(4,1)} %bitcast.32), calls=%async_computation.3 | async-start | bytes 458752
  202.0 13.7 %copy-start.3 = (f32[8,1,8,1,128,1]{4,2,0,5,3,1:T(8,128)S(1)}, f32[8,1,8,1,128,1]{4,2,0,5,3,1:T(8,128)}, u32[]{:S(2)}) copy-start(f32[8,1,8,1,128,1]{4,2,0,5,3,1:T(8,128)} %copy.64) | copy-start | bytes 98308
  223.4 148.1 %all-reduce.8.cloned.1.call-start = ((), (), s32[]{:S(2)}) async-start(), calls=%async_computation.1 | async-start | bytes 131072 | tf_op jit(solution)/shard_map/psum | solution.py:58
Sparse Core Ops, SparseCore 0:
  223.5 86.6 all-reduce.5
  312.5 58.8 all-reduce.7
